TPU v7x, 32 devices: a whole 2x2x4 slice. The times are simulated.
32 devices in a mesh: parts: 1, head: 32 (over z, y, x, core).
Axes of the slice: x: 2, y: 2, z: 4, core: 2. Of those that a mesh axis runs over, the one named last changes fastest.
Arguments:
- queries: bfloat16 [8, 2048, 2048], P('parts', 'head'), may hold values from -6 to 6
- keys: bfloat16 [8, 2048, 2048], P('parts', 'head'), may hold values from -6 to 6
- values: bfloat16 [8, 2048, 2048], P('parts', 'head'), may hold values from -6 to 6
- slot_positions: int32 [8, 2048], P('parts', 'head'), may hold values from 0 to 2047, each once within a row
- counts: int32 [8], P('parts'), may hold values from 16 to 2048, as said below
- timesteps: int32 [8], P('parts'), may hold values from 0 to 999
- labels: int32 [8], P('parts'), may hold values from 0 to 127
- time_weight: bfloat16 [256, 4096], replicated, may hold values from -0.375 to 0.375
- norm_gain: float32 [2048], replicated, may hold values from 0.25 to 1.75
- gate_weight: bfloat16 [2048, 8192], P(None, 'head'), may hold values from -0.125 to 0.125
- up_weight: bfloat16 [2048, 8192], P(None, 'head'), may hold values from -0.125 to 0.125
- down_weight: bfloat16 [8192, 2048], P('head'), may hold values from -0.0625 to 0.0625
- class_weight: bfloat16 [2048, 128], replicated, may hold values from -3 to 3
- class_bias: float32 [128], replicated, may hold values from -5 to 112
Outputs:
- attention: bfloat16 [256, 2048, 64], P(('parts', 'head'))
- guidance: float32 [8, 128, 2048], P('parts', 'head')
Inputs may be any that keep to these rules, and one draw needn't show every extreme that they name: `counts`: multiples of 16; in every part one shower has exactly 2048. `slot_positions`: each shower's row is a permutation of 0 to 2047.
All inputs are finite; a program needn't handle non-finite values.
Results may differ from a plain program's by a relative error of at most 0.01.
The roundings to bfloat16 on the way count: a program that leaves them out, or rounds other values in their place, can miss the bound.
Values may be sent and summed in bfloat16 or wider, within the bound.
A program may use at most 192 MiB of HBM per device.

v0:
```python
import math
import jax
import jax.numpy as jnp
from jax import lax
from jax.sharding import PartitionSpec as P

HEADS = 32
POOL = 16
epsilon = 1e-06


def sinusoid(steps, embed_width):
    half_width = embed_width // 2
    frequency = jnp.exp(-math.log(10000.0) * jnp.arange(half_width, dtype=jnp.float32) / half_width)
    angles = steps.astype(jnp.float32)[:, None] * frequency[None, :]
    return jnp.concatenate([jnp.cos(angles), jnp.sin(angles)], axis=1)


def attend_pair(pair_data):
    query_rows, key_rows, value_rows, key_valid = pair_data
    head_dim = query_rows.shape[1]
    scores = jnp.dot(query_rows, key_rows.T, preferred_element_type=jnp.float32) * head_dim ** (
        -0.5
    )
    scores = jnp.where(key_valid[None, :], scores, -jnp.inf)
    peak = jnp.max(scores, axis=1, keepdims=True)
    exponent = jnp.exp(scores - peak)
    weights = (exponent / jnp.sum(exponent, axis=1, keepdims=True)).astype(jnp.bfloat16)
    mixed = jnp.dot(weights, value_rows, preferred_element_type=jnp.float32)
    return (mixed * key_valid[:, None].astype(jnp.float32)).astype(jnp.bfloat16)


def body(
    queries,
    keys,
    values,
    slot_positions,
    counts,
    timesteps,
    labels,
    time_weight,
    norm_gain,
    gate_weight,
    up_weight,
    down_weight,
    class_weight,
    class_bias,
):
    devices = lax.axis_size("head")
    device_index = lax.axis_index("head")
    showers, local_length, model_width = queries.shape
    head_dim = model_width // HEADS
    pairs_here = showers * HEADS // devices
    windows = local_length * devices // POOL
    per_device = windows // devices
    row_total = showers * windows

    def to_pairs(block):
        return (
            block.reshape(showers, local_length, HEADS, head_dim)
            .transpose(0, 2, 1, 3)
            .reshape(devices, pairs_here, local_length, head_dim)
        )

    valid_slots = slot_positions < counts[:, None]
    slot_flags = jnp.broadcast_to(
        valid_slots.astype(jnp.bfloat16)[:, None, :], (showers, HEADS, local_length)
    ).reshape(devices, pairs_here, local_length)
    query_rows = lax.all_to_all(to_pairs(queries), "head", split_axis=0, concat_axis=2, tiled=True)
    key_rows = lax.all_to_all(to_pairs(keys), "head", split_axis=0, concat_axis=2, tiled=True)
    value_rows = lax.all_to_all(to_pairs(values), "head", split_axis=0, concat_axis=2, tiled=True)
    flag_rows = lax.all_to_all(slot_flags, "head", split_axis=0, concat_axis=2, tiled=True)
    pair_count = query_rows.shape[1]
    flag_rows = flag_rows[0]
    attention_part = lax.map(
        attend_pair, (query_rows[0], key_rows[0], value_rows[0], flag_rows > 0.5)
    )
    flag_values = flag_rows.astype(jnp.float32)
    window_count = jnp.sum(flag_values.reshape(pair_count, windows, POOL), axis=2)
    window_sum = jnp.sum(
        attention_part.astype(jnp.float32).reshape(pair_count, windows, POOL, head_dim), axis=2
    )
    pooled_part = (window_sum / jnp.maximum(window_count, 1.0)[:, :, None]).astype(jnp.bfloat16)
    attention, pooled, window_count = (
        attention_part,
        pooled_part,
        window_count.astype(jnp.bfloat16),
    )
    pooled_all, count_all = (
        lax.all_gather(pooled, "head", axis=0, tiled=True),
        lax.all_gather(window_count, "head", axis=0, tiled=True),
    )
    pooled_rows = (
        pooled_all.reshape(showers, HEADS, devices, per_device, head_dim)
        .transpose(2, 0, 3, 1, 4)
        .reshape(devices, showers, per_device, model_width)
        .astype(jnp.float32)
    )
    row_count = (
        count_all.reshape(showers, HEADS, devices, per_device)[:, 0]
        .transpose(1, 0, 2)
        .astype(jnp.float32)
    )
    embedding = sinusoid(timesteps, time_weight.shape[0]).astype(jnp.bfloat16)
    modulation = jnp.dot(embedding, time_weight, preferred_element_type=jnp.float32)
    shifts = modulation[:, None, :model_width]
    scales = 1.0 + modulation[:, None, model_width:]
    inverse_rms = lax.rsqrt(jnp.mean(pooled_rows * pooled_rows, axis=3, keepdims=True) + epsilon)
    unit_rows = pooled_rows * inverse_rms
    normed = (
        (unit_rows * norm_gain * scales[None] + shifts[None])
        .astype(jnp.bfloat16)
        .reshape(row_total, model_width)
    )
    own_pooled = lax.dynamic_slice_in_dim(pooled_rows, device_index, 1, 0)[0]
    own_count = lax.dynamic_slice_in_dim(row_count, device_index, 1, 0)[0]
    own_units = lax.dynamic_slice_in_dim(unit_rows, device_index, 1, 0)[0]
    own_inverse = lax.dynamic_slice_in_dim(inverse_rms, device_index, 1, 0)[0]
    shower_counts = counts.astype(jnp.float32)
    class_matrix = class_weight.astype(jnp.float32)
    target = (
        labels[:, None] == jnp.arange(class_matrix.shape[1], dtype=jnp.int32)[None, :]
    ).astype(jnp.float32)
    gate_out = jnp.dot(normed, gate_weight, preferred_element_type=jnp.float32)
    up_out = jnp.dot(normed, up_weight, preferred_element_type=jnp.float32)
    activated = jax.nn.silu(gate_out)
    hidden = (activated * up_out).astype(jnp.bfloat16)
    own_mlp = lax.psum_scatter(
        jnp.dot(hidden, down_weight, preferred_element_type=jnp.float32),
        "head",
        scatter_dimension=0,
        tiled=True,
    ).reshape(showers, per_device, model_width)
    partial_value = jnp.sum(own_count[:, :, None] * (own_pooled + own_mlp), axis=1)
    features = lax.psum(partial_value, "head") / shower_counts[:, None]
    logits = jnp.dot(features, class_matrix, precision=lax.Precision.HIGHEST) + class_bias
    exponent = jnp.exp(logits - jnp.max(logits, axis=1, keepdims=True))
    probability = exponent / jnp.sum(exponent, axis=1, keepdims=True)
    feature_grad = jnp.dot(target - probability, class_matrix.T, precision=lax.Precision.HIGHEST)
    row_grads = (
        row_count[:, :, :, None]
        / shower_counts[None, :, None, None]
        * feature_grad[None, :, None, :]
    )
    hidden_grad = jnp.dot(
        row_grads.astype(jnp.bfloat16).reshape(row_total, model_width),
        down_weight.T,
        preferred_element_type=jnp.float32,
    )
    sigmoid_gate = jax.nn.sigmoid(gate_out)
    gate_grad = (
        hidden_grad * up_out * sigmoid_gate * (1.0 + gate_out * (1.0 - sigmoid_gate))
    ).astype(jnp.bfloat16)
    up_grad = (hidden_grad * activated).astype(jnp.bfloat16)
    normed_grad = lax.psum_scatter(
        jnp.dot(gate_grad, gate_weight.T, preferred_element_type=jnp.float32)
        + jnp.dot(up_grad, up_weight.T, preferred_element_type=jnp.float32),
        "head",
        scatter_dimension=0,
        tiled=True,
    ).reshape(showers, per_device, model_width)
    own_row_grads = lax.dynamic_slice_in_dim(row_grads, device_index, 1, 0)[0]
    unit_grad = normed_grad * norm_gain * scales
    pooled_grad = own_inverse * (
        unit_grad - own_units * jnp.mean(unit_grad * own_units, axis=2, keepdims=True)
    )
    guidance = windows * (own_row_grads + pooled_grad)
    return (attention, guidance)


def solution(mesh):
    in_specs = (
        P("parts", "head", None),
        P("parts", "head", None),
        P("parts", "head", None),
        P("parts", "head"),
        P("parts"),
        P("parts"),
        P("parts"),
        P(),
        P(),
        P(None, "head"),
        P(None, "head"),
        P("head", None),
        P(),
        P(),
    )
    out_specs = (P(("parts", "head"), None, None), P("parts", "head", None))
    return jax.shard_map(body, mesh=mesh, in_specs=in_specs, out_specs=out_specs, check_vma=False)
```

profile of v0, /device:TPU:0, one launch (start us, length us, event | category | flops | bytes accessed | tf_op | source)
XLA Modules:
  0.0 928.5 jit_solution(15136962674087946436)
XLA Ops:
  8.8 7.3 all-to-all-start
  16.2 7.1 reshape.154
  23.3 5.8 copy.119
  29.0 7.9 reshape.178
  36.9 6.0 all-to-all-start.1
  42.9 7.1 reshape.156
  50.0 5.7 copy.121
  55.7 7.9 reshape.180
  63.6 28.0 %all-to-all-done.1 = bf16[32,2,16384]{2,1,0:T(2,128)(2,1)} async-done(((bf16[32,2,16384]{2,1,0:T(2,128)(2,1)}), bf16[32,2,16384]{2,1,0:T(2,128)(2,1)}, u32[]{:S(2)}, u32[]{:S(2)}) %all-to-all-start.1) | async-done | bytes 2097184 | tf_op jit(solution)/shard_map/all_to_all | solution.py:69
  96.0 7.1 reshape.158
  103.1 5.7 copy.123
  108.8 7.9 reshape.182
  116.7 28.0 %all-to-all-done.2 = bf16[32,2,16384]{2,1,0:T(2,128)(2,1)} async-done(((bf16[32,2,16384]{2,1,0:T(2,128)(2,1)}), bf16[32,2,16384]{2,1,0:T(2,128)(2,1)}, u32[]{:S(2)}, u32[]{:S(2)}) %all-to-all-start.2) | async-done | bytes 2097184 | tf_op jit(solution)/shard_map/all_to_all | solution.py:70
  150.3 7.9 reshape.179
  158.3 5.5 copy.144
  163.8 7.9 reshape.181
  171.7 5.5 copy.145
  177.2 20.4 %all-to-all-done.3 = bf16[32,2,16384]{2,1,0:T(2,128)(2,1)} async-done(((bf16[32,2,16384]{2,1,0:T(2,128)(2,1)}), bf16[32,2,16384]{2,1,0:T(2,128)(2,1)}, u32[]{:S(2)}, u32[]{:S(2)}) %all-to-all-start.3) | async-done | bytes 2097184 | tf_op jit(solution)/shard_map/all_to_all | solution.py:71
  197.6 7.9 reshape.183
  205.6 5.5 copy.146
  211.1 119.2 %while.10 = (s32[]{:T(128)}, bf16[8,2048,64]{1,2,0:T(8,128)(2,1)}, pred[8,2048]{1,0:T(8,128)(4,1)S(1)}, bf16[8,2048,64]{2,1,0:T(8,128)(2,1)}, bf16[8,2048,64]{2,...) while((s32[]{:T(128)}, bf16[8,2048,64]{1,2,0:T(8,128)(2,1)}, pred[8,2048]{1,0:T(8,128)(4,1)S(1)}, ...), condition=%wide.region_3.4_spmd, body=%wide.region_0.3_spmd.sunk | while | flops 1124333568 | bytes 52238416 | solution.py:75
  220.2 6.0 fusion.77
  235.0 6.0 fusion.77
  249.9 6.0 fusion.77
  264.8 6.0 fusion.77
  279.6 6.0 fusion.77
  294.5 6.0 fusion.77
  309.4 6.0 fusion.77
  324.3 6.0 fusion.77
  330.3 5.7 copy.133
  336.0 5.4 bitcast_reduce_fusion
  343.1 5.3 mul.174
  348.5 10.4 %mul.175 = f32[1024,2048]{1,0:T(8,128)} reshape(f32[32,8,4,2048]{3,2,1,0:T(4,128)} %mul.174) | data formatting | bytes 16777216 | tf_op jit(solution)/shard_map/mul | solution.py:111
  358.8 5.3 add.82
  364.2 10.0 %add.83 = f32[1024,2048]{1,0:T(8,128)} reshape(f32[32,8,4,2048]{3,2,1,0:T(4,128)} %add.82) | data formatting | bytes 16777216 | tf_op jit(solution)/shard_map/add | solution.py:111
  374.2 29.7 %all-gather.2.cloned.1.call-done = bf16[256,128,64]{1,2,0:T(8,128)(2,1)} async-done(((bf16[8,128,64]{1,2,0:T(8,128)(2,1)}), bf16[256,128,64]{1,2,0:T(8,128)(2,1)}) %all-gather.2.cloned.1.call-update) | async-done | bytes 4194320 | tf_op jit(solution)/shard_map/all_gather | solution.py:90
  409.5 12.7 %copy.135 = f32[256,128,64]{2,0,1:T(8,128)} copy(bf16[256,128,64]{1,2,0:T(8,128)(2,1)} %all-gather.2.cloned.1.call-done) | data formatting | bytes 12582912 | tf_op jit(solution)/shard_map/convert_element_type | solution.py:97
  422.2 11.9 %copy.137 = f32[32,8,4,32,64]{4,3,2,1,0:T(8,128)} copy(f32[32,8,4,32,64]{4,3,1,2,0:T(8,128)} %bitcast.115) | data formatting | bytes 16777216 | tf_op jit(solution)/shard_map/convert_element_type | solution.py:97
  434.0 14.8 %reshape.169 = f32[1024,2048]{1,0:T(8,128)} reshape(f32[32,8,4,32,64]{4,3,2,1,0:T(8,128)} %copy.137) | data formatting | bytes 16777216 | tf_op jit(solution)/shard_map/convert_element_type | solution.py:97
  448.9 10.4 %add_convert_fusion = bf16[1024,2048]{1,0:T(8,128)(2,1)S(1)} fusion(f32[1024,2048]{1,0:T(8,128)} %add.83, f32[1024,2048]{1,0:T(8,128)} %mul.175, f32[1024,2048]{1,0:T(8,128)} %reshape.169, f32[2048]{0:T(1024)S(1)} %copy-done.8, f32[1024]{0:T(1024)S(1)} %rsqrt.18), kind=kLoop, calls=%fused_computation.24 | loop fusion | flops 10485760 | bytes 29372416 | tf_op jit(solution)/shard_map/convert_element_type | solution.py:112
  467.4 39.9 %all_gather.6 = bf16[256,128]{1,0:T(8,128)(2,1)S(1)} all-gather(bf16[8,128]{1,0:T(8,128)(2,1)S(1)} %copy-done.10), channel_id=1, replica_groups=mesh['parts'=1,'head'=32] {'head'}, dimensions={0}, use_global_device_ids=true | all-gather | bytes 67584 | tf_op jit(solution)/shard_map/all_gather | solution.py:91
  512.9 14.9 %reshape.168 = f32[32,8,4,2048]{3,1,2,0:T(8,128)} reshape(f32[32,8,4,32,64]{4,3,1,2,0:T(8,128)} %bitcast.116) | data formatting | bytes 16777216 | tf_op jit(solution)/shard_map/convert_element_type | solution.py:97
  529.4 87.2 %reduce-scatter.3.cloned.1.call-done = f32[32,2048]{1,0:T(8,128)} async-done(((f32[1024,2048]{1,0:T(8,128)}), f32[32,2048]{1,0:T(8,128)}) %reduce-scatter.3.cloned.1.call-update) | async-done | bytes 262160 | tf_op jit(solution)/shard_map/reduce_scatter | solution.py:128
  623.0 114.5 %all-reduce.2.cloned.1.call-done = f32[8,2048]{1,0:T(8,128)} async-done(((f32[8,2048]{1,0:T(8,128)}), f32[8,2048]{1,0:T(8,128)}) %all-reduce.2.cloned.1.call-update) | async-done | bytes 65552 | tf_op jit(solution)/shard_map/psum | solution.py:135
  740.9 5.4 mul.180
  746.2 10.2 %mul.186 = f32[1024,2048]{1,0:T(8,128)} reshape(f32[32,8,4,2048]{3,2,1,0:T(4,128)} %mul.180) | data formatting | bytes 16777216 | tf_op jit(solution)/shard_map/mul | solution.py:141
  756.4 5.1 fusion.18
  769.1 150.3 %reduce-scatter.5.cloned.1.call-done = f32[32,2048]{1,0:T(8,128)} async-done(((f32[1024,2048]{1,0:T(8,128)}), f32[32,2048]{1,0:T(8,128)}) %reduce-scatter.5.cloned.1.call-update) | async-done | bytes 262160 | tf_op jit(solution)/shard_map/reduce_scatter | solution.py:155
  (126 shorter events, 124.3 us)
Async XLA Ops:
  7.2 335.5 %copy-start = (bf16[256,4096]{1,0:T(8,128)(2,1)S(1)}, bf16[256,4096]{1,0:T(8,128)(2,1)}, u32[]{:S(2)}) copy-start(bf16[256,4096]{1,0:T(8,128)(2,1)} %param.23) | copy-start | bytes 6291460
  8.8 28.1 %all-to-all-start = ((bf16[32,2,256]{2,1,0:T(2,128)(2,1)}), bf16[32,2,256]{2,1,0:T(2,128)(2,1)S(1)}, u32[]{:S(2)}, u32[]{:S(2)}) async-start(bf16[32,2,256]{2,1,0:T(2,128)(2,1)} %reshape.176), calls=%async_computation | async-start | bytes 65536 | tf_op jit(solution)/shard_map/all_to_all | solution.py:72
  36.9 54.7 %all-to-all-start.1 = ((bf16[32,2,16384]{2,1,0:T(2,128)(2,1)}), bf16[32,2,16384]{2,1,0:T(2,128)(2,1)}, u32[]{:S(2)}, u32[]{:S(2)}) async-start(bf16[32,2,16384]{2,1,0:T(2,128)(2,1)} %reshape.178), calls=%async_computation.1 | async-start | bytes 4194304 | tf_op jit(solution)/shard_map/all_to_all | solution.py:69
  91.6 53.1 %all-to-all-start.2 = ((bf16[32,2,16384]{2,1,0:T(2,128)(2,1)}), bf16[32,2,16384]{2,1,0:T(2,128)(2,1)}, u32[]{:S(2)}, u32[]{:S(2)}) async-start(bf16[32,2,16384]{2,1,0:T(2,128)(2,1)} %reshape.180), calls=%async_computation.2 | async-start | bytes 4194304 | tf_op jit(solution)/shard_map/all_to_all | solution.py:70
  144.7 52.9 %all-to-all-start.3 = ((bf16[32,2,16384]{2,1,0:T(2,128)(2,1)}), bf16[32,2,16384]{2,1,0:T(2,128)(2,1)}, u32[]{:S(2)}, u32[]{:S(2)}) async-start(bf16[32,2,16384]{2,1,0:T(2,128)(2,1)} %reshape.182), calls=%async_computation.3 | async-start | bytes 4194304 | tf_op jit(solution)/shard_map/all_to_all | solution.py:71
  148.9 255.0 %all-gather.2.cloned.1.call-start = ((), (), s32[]{:S(2)}) async-start(), calls=%async_computation.6 | async-start | bytes 4325376 | tf_op jit(solution)/shard_map/all_gather | solution.py:90
  330.3 11.2 %copy-start.9 = (f32[8,128]{1,0:T(8,128)S(1)}, f32[8,128]{1,0:T(8,128)}, u32[]{:S(2)}) copy-start(f32[8,128]{1,0:T(8,128)} %get-tuple-element.86) | copy-start | bytes 12292
  330.3 12.3 %copy-start.12 = (s32[8]{0:T(128)S(1)}, s32[8]{0:T(128)}, u32[]{:S(2)}) copy-start(s32[8]{0:T(128)} %param.21) | copy-start | bytes 100
  342.5 274.2 %reduce-scatter.3.cloned.1.call-start = ((), (), s32[]{:S(2)}) async-start(), calls=%async_computation.7 | async-start | bytes 8650752 | tf_op jit(solution)/shard_map/reduce_scatter | solution.py:128
  434.0 14.8 %copy-start.8 = (f32[2048]{0:T(1024)S(1)}, f32[2048]{0:T(1024)}, u32[]{:S(2)}) copy-start(f32[2048]{0:T(1024)} %param.24) | copy-start | bytes 24580
  448.9 10.4 %copy-start.4 = (bf16[2048,256]{1,0:T(8,128)(2,1)S(1)}, bf16[2048,256]{1,0:T(8,128)(2,1)}, u32[]{:S(2)}) copy-start(bf16[2048,256]{1,0:T(8,128)(2,1)} %param.25) | copy-start | bytes 3145732
  448.9 11.7 %copy-start.6 = (bf16[2048,256]{1,0:T(8,128)(2,1)S(1)}, bf16[2048,256]{1,0:T(8,128)(2,1)}, u32[]{:S(2)}) copy-start(bf16[2048,256]{1,0:T(8,128)(2,1)} %param.26) | copy-start | bytes 3145732
  459.3 3.5 copy-start.3
  461.8 1.0 copy-start.1
  462.8 4.6 copy-start.11
  462.8 4.6 copy-start.10
  467.4 270.2 %all-reduce.2.cloned.1.call-start = ((), (), s32[]{:S(2)}) async-start(), calls=%async_computation.8 | async-start | bytes 131072 | tf_op jit(solution)/shard_map/psum | solution.py:135
  620.4 299.0 %reduce-scatter.5.cloned.1.call-start = ((), (), s32[]{:S(2)}) async-start(), calls=%async_computation.9 | async-start | bytes 8650752 | tf_op jit(solution)/shard_map/reduce_scatter | solution.py:155
  756.4 5.1 copy-start.2
  756.4 5.1 copy-start.5
  761.5 1.5 copy-start.7
Sparse Core Ops, SparseCore 0:
  342.6 61.2 all-gather.1
  467.5 149.1 reduce-scatter.2
  622.2 115.2 all-reduce.1
  767.8 151.5 reduce-scatter.4
where the time goes:
time: 940 us; the launch traced here: 929 us
  waiting for transfers between devices  458 us (49%)
  local copies, waits for them, and re-layouts  224 us (24%)
  matrix products  99.8 us (11%)
  other arithmetic  70.1 us (7%)
  blocking collectives  39.9 us (4%)
  starting transfers between devices  22.1 us (2%)
  between operations  14.4 us (2%)
    reduce_scatter x1, waiting for transfers between devices, body(): lax.psum_scatter(jnp.dot(gate_grad, gate_weight.T, preferred_element_type...  150 us
    psum x1, waiting for transfers between devices, body(): features = lax.psum(partial_value, 'head') / shower_counts[:, None]  114 us
    reduce_scatter x1, waiting for transfers between devices, body(): lax.psum_scatter(jnp.dot(hidden, down_weight, preferred_element_type=jnp....  87.2 us
    convert_element_type x4, local copies, waits for them, and re-layouts, body(): pooled_rows = pooled_all.reshape(showers, HEADS, devices, per_device, hea...  54.3 us
    unnamed x34, local copies, waits for them, and re-layouts  49.3 us
    dot_general x8, matrix products, attend_pair(): mixed = jnp.dot(weights, value_rows, preferred_element_type=jnp.float32)  48.2 us
    reduce_sum x8, other arithmetic, attend_pair(): jnp.sum(exponent, axis=1, keepdims=True)  40.4 us
    all_gather x1, blocking collectives, body(): lax.all_gather(window_count, 'head', axis=0, tiled=True)  39.9 us
  transfers between devices with their start and end apart: 8, of which 7 were waited for; matrix products, arithmetic and copies ran while one was open for 16% of the time, Pallas kernels for 0%

commit v1 on v0

--- a/solution.py
+++ b/solution.py
@@ -132,7 +132,7 @@
         tiled=True,
     ).reshape(showers, per_device, model_width)
     partial_value = jnp.sum(own_count[:, :, None] * (own_pooled + own_mlp), axis=1)
-    features = lax.psum(partial_value, "head") / shower_counts[:, None]
+    features = jnp.sum(lax.all_gather(partial_value, "head"), axis=0) / shower_counts[:, None]
     logits = jnp.dot(features, class_matrix, precision=lax.Precision.HIGHEST) + class_bias
     exponent = jnp.exp(logits - jnp.max(logits, axis=1, keepdims=True))
     probability = exponent / jnp.sum(exponent, axis=1, keepdims=True)

time: 940 us -> 874 us (0.930)
  waiting for transfers between devices: 458 us -> 392 us
    psum x1 -> x0, waiting for transfers between devices: 114 us -> none  [body(): features = lax.psum(partial_value, 'head') / shower_counts[:, None]]
    all_gather x0 -> x1, waiting for transfers between devices: none -> 48.9 us  [body(): lax.all_gather(partial_value, 'head')]
    unnamed x34 -> x36, local copies, waits for them, and re-layouts: 49.3 us -> 50.1 us
  transfers between devices with their start and end apart: 8 -> 8, of which waited for: 7 -> 7; matrix products, arithmetic and copies ran while one was open for 16% -> 17% of each run, Pallas kernels for 0% -> 0%
where the time goes in v1:
time: 874 us; the launch traced here: 862 us
  waiting for transfers between devices  392 us (45%)
  local copies, waits for them, and re-layouts  223 us (26%)
  matrix products  99.8 us (11%)
  other arithmetic  70.3 us (8%)
  blocking collectives  39.8 us (5%)
  starting transfers between devices  22.1 us (3%)
  between operations  14.4 us (2%)
    reduce_scatter x1, waiting for transfers between devices, body(): lax.psum_scatter(jnp.dot(gate_grad, gate_weight.T, preferred_element_type...  147 us
    reduce_scatter x1, waiting for transfers between devices, body(): lax.psum_scatter(jnp.dot(hidden, down_weight, preferred_element_type=jnp....  90.1 us
    convert_element_type x4, local copies, waits for them, and re-layouts, body(): pooled_rows = pooled_all.reshape(showers, HEADS, devices, per_device, hea...  54.3 us
    unnamed x36, local copies, waits for them, and re-layouts  50.1 us
    all_gather x1, waiting for transfers between devices, body(): lax.all_gather(partial_value, 'head')  48.9 us
    dot_general x8, matrix products, attend_pair(): mixed = jnp.dot(weights, value_rows, preferred_element_type=jnp.float32)  48.2 us
    reduce_sum x8, other arithmetic, attend_pair(): jnp.sum(exponent, axis=1, keepdims=True)  40.4 us
    all_gather x1, blocking collectives, body(): lax.all_gather(window_count, 'head', axis=0, tiled=True)  39.8 us
  transfers between devices with their start and end apart: 8, of which 7 were waited for; matrix products, arithmetic and copies ran while one was open for 17% of the time, Pallas kernels for 0%

profile of v1, /device:TPU:0, one launch (start us, length us, event | category | flops | bytes accessed | tf_op | source)
XLA Modules:
  0.0 862.4 jit_solution(2568856933649873889)
XLA Ops:
  8.8 7.3 all-to-all-start
  16.2 7.1 reshape.154
  23.3 5.8 copy.145
  29.0 7.9 reshape.179
  36.9 6.0 all-to-all-start.1
  42.9 7.1 reshape.156
  50.0 5.7 copy.147
  55.7 7.9 reshape.181
  63.6 28.0 %all-to-all-done.1 = bf16[32,2,16384]{2,1,0:T(2,128)(2,1)} async-done(((bf16[32,2,16384]{2,1,0:T(2,128)(2,1)}), bf16[32,2,16384]{2,1,0:T(2,128)(2,1)}, u32[]{:S(2)}, u32[]{:S(2)}) %all-to-all-start.1) | async-done | bytes 2097184 | tf_op jit(solution)/shard_map/all_to_all | solution.py:69
  96.0 7.1 reshape.158
  103.1 5.7 copy.149
  108.8 7.9 reshape.183
  116.7 28.0 %all-to-all-done.2 = bf16[32,2,16384]{2,1,0:T(2,128)(2,1)} async-done(((bf16[32,2,16384]{2,1,0:T(2,128)(2,1)}), bf16[32,2,16384]{2,1,0:T(2,128)(2,1)}, u32[]{:S(2)}, u32[]{:S(2)}) %all-to-all-start.2) | async-done | bytes 2097184 | tf_op jit(solution)/shard_map/all_to_all | solution.py:70
  150.3 8.0 reshape.180
  158.3 5.5 copy.170
  163.8 7.9 reshape.182
  171.7 5.5 copy.171
  177.2 20.4 %all-to-all-done.3 = bf16[32,2,16384]{2,1,0:T(2,128)(2,1)} async-done(((bf16[32,2,16384]{2,1,0:T(2,128)(2,1)}), bf16[32,2,16384]{2,1,0:T(2,128)(2,1)}, u32[]{:S(2)}, u32[]{:S(2)}) %all-to-all-start.3) | async-done | bytes 2097184 | tf_op jit(solution)/shard_map/all_to_all | solution.py:71
  197.6 8.0 reshape.184
  205.6 5.5 copy.172
  211.1 119.2 %while.10 = (s32[]{:T(128)}, bf16[8,2048,64]{1,2,0:T(8,128)(2,1)}, pred[8,2048]{1,0:T(8,128)(4,1)S(1)}, bf16[8,2048,64]{2,1,0:T(8,128)(2,1)}, bf16[8,2048,64]{2,...) while((s32[]{:T(128)}, bf16[8,2048,64]{1,2,0:T(8,128)(2,1)}, pred[8,2048]{1,0:T(8,128)(4,1)S(1)}, ...), condition=%wide.region_3.4_spmd, body=%wide.region_0.3_spmd.sunk | while | flops 1124333568 | bytes 52238416 | solution.py:75
  220.1 6.0 fusion.77
  235.0 6.0 fusion.77
  249.9 6.0 fusion.77
  264.8 6.0 fusion.77
  279.6 6.0 fusion.77
  294.5 6.0 fusion.77
  309.4 6.0 fusion.77
  324.2 6.0 fusion.77
  330.3 5.7 copy.159
  336.0 5.4 bitcast_reduce_fusion
  343.1 5.3 mul.174
  348.4 10.4 %mul.175 = f32[1024,2048]{1,0:T(8,128)} reshape(f32[32,8,4,2048]{3,2,1,0:T(4,128)} %mul.174) | data formatting | bytes 16777216 | tf_op jit(solution)/shard_map/mul | solution.py:111
  358.8 5.3 add.80
  364.2 10.0 %add.81 = f32[1024,2048]{1,0:T(8,128)} reshape(f32[32,8,4,2048]{3,2,1,0:T(4,128)} %add.80) | data formatting | bytes 16777216 | tf_op jit(solution)/shard_map/add | solution.py:111
  374.2 29.7 %all-gather.4.cloned.1.call-done = bf16[256,128,64]{1,2,0:T(8,128)(2,1)} async-done(((bf16[8,128,64]{1,2,0:T(8,128)(2,1)}), bf16[256,128,64]{1,2,0:T(8,128)(2,1)}) %all-gather.4.cloned.1.call-update) | async-done | bytes 4194320 | tf_op jit(solution)/shard_map/all_gather | solution.py:90
  409.5 12.8 %copy.161 = f32[256,128,64]{2,0,1:T(8,128)} copy(bf16[256,128,64]{1,2,0:T(8,128)(2,1)} %all-gather.4.cloned.1.call-done) | data formatting | bytes 12582912 | tf_op jit(solution)/shard_map/convert_element_type | solution.py:97
  422.2 11.9 %copy.163 = f32[32,8,4,32,64]{4,3,2,1,0:T(8,128)} copy(f32[32,8,4,32,64]{4,3,1,2,0:T(8,128)} %bitcast.117) | data formatting | bytes 16777216 | tf_op jit(solution)/shard_map/convert_element_type | solution.py:97
  434.1 14.8 %reshape.169 = f32[1024,2048]{1,0:T(8,128)} reshape(f32[32,8,4,32,64]{4,3,2,1,0:T(8,128)} %copy.163) | data formatting | bytes 16777216 | tf_op jit(solution)/shard_map/convert_element_type | solution.py:97
  448.9 10.4 %add_convert_fusion = bf16[1024,2048]{1,0:T(8,128)(2,1)S(1)} fusion(f32[1024,2048]{1,0:T(8,128)} %add.81, f32[1024,2048]{1,0:T(8,128)} %mul.175, f32[1024,2048]{1,0:T(8,128)} %reshape.169, f32[2048]{0:T(1024)S(1)} %copy-done.9, f32[1024]{0:T(1024)S(1)} %rsqrt.18), kind=kLoop, calls=%fused_computation.24 | loop fusion | flops 10485760 | bytes 29372416 | tf_op jit(solution)/shard_map/convert_element_type | solution.py:112
  467.5 39.8 %all_gather.12 = bf16[256,128]{1,0:T(8,128)(2,1)S(1)} all-gather(bf16[8,128]{1,0:T(8,128)(2,1)S(1)} %copy-done.11), channel_id=1, replica_groups=mesh['parts'=1,'head'=32] {'head'}, dimensions={0}, use_global_device_ids=true | all-gather | bytes 67584 | tf_op jit(solution)/shard_map/all_gather | solution.py:91
  510.1 14.9 %reshape.168 = f32[32,8,4,2048]{3,1,2,0:T(8,128)} reshape(f32[32,8,4,32,64]{4,3,1,2,0:T(8,128)} %bitcast.118) | data formatting | bytes 16777216 | tf_op jit(solution)/shard_map/convert_element_type | solution.py:97
  526.6 90.1 %reduce-scatter.3.cloned.1.call-done = f32[32,2048]{1,0:T(8,128)} async-done(((f32[1024,2048]{1,0:T(8,128)}), f32[32,2048]{1,0:T(8,128)}) %reduce-scatter.3.cloned.1.call-update) | async-done | bytes 262160 | tf_op jit(solution)/shard_map/reduce_scatter | solution.py:128
  623.7 48.9 %all-gather.6.cloned.1.call-done = f32[256,2048]{1,0:T(8,128)} async-done(((f32[8,2048]{1,0:T(8,128)}), f32[256,2048]{1,0:T(8,128)}) %all-gather.6.cloned.1.call-update) | async-done | bytes 2097168 | tf_op jit(solution)/shard_map/all_gather | solution.py:135
  677.7 5.4 mul.180
  683.1 10.2 %mul.186 = f32[1024,2048]{1,0:T(8,128)} reshape(f32[32,8,4,2048]{3,2,1,0:T(4,128)} %mul.180) | data formatting | bytes 16777216 | tf_op jit(solution)/shard_map/mul | solution.py:141
  693.2 5.1 fusion.18
  706.0 147.3 %reduce-scatter.5.cloned.1.call-done = f32[32,2048]{1,0:T(8,128)} async-done(((f32[1024,2048]{1,0:T(8,128)}), f32[32,2048]{1,0:T(8,128)}) %reduce-scatter.5.cloned.1.call-update) | async-done | bytes 262160 | tf_op jit(solution)/shard_map/reduce_scatter | solution.py:155
  (129 shorter events, 123.9 us)
Async XLA Ops:
  7.2 335.5 %copy-start = (bf16[256,4096]{1,0:T(8,128)(2,1)S(1)}, bf16[256,4096]{1,0:T(8,128)(2,1)}, u32[]{:S(2)}) copy-start(bf16[256,4096]{1,0:T(8,128)(2,1)} %param.23) | copy-start | bytes 6291460
  8.8 28.1 %all-to-all-start = ((bf16[32,2,256]{2,1,0:T(2,128)(2,1)}), bf16[32,2,256]{2,1,0:T(2,128)(2,1)S(1)}, u32[]{:S(2)}, u32[]{:S(2)}) async-start(bf16[32,2,256]{2,1,0:T(2,128)(2,1)} %reshape.177), calls=%async_computation | async-start | bytes 65536 | tf_op jit(solution)/shard_map/all_to_all | solution.py:72
  36.9 54.7 %all-to-all-start.1 = ((bf16[32,2,16384]{2,1,0:T(2,128)(2,1)}), bf16[32,2,16384]{2,1,0:T(2,128)(2,1)}, u32[]{:S(2)}, u32[]{:S(2)}) async-start(bf16[32,2,16384]{2,1,0:T(2,128)(2,1)} %reshape.179), calls=%async_computation.1 | async-start | bytes 4194304 | tf_op jit(solution)/shard_map/all_to_all | solution.py:69
  91.6 53.1 %all-to-all-start.2 = ((bf16[32,2,16384]{2,1,0:T(2,128)(2,1)}), bf16[32,2,16384]{2,1,0:T(2,128)(2,1)}, u32[]{:S(2)}, u32[]{:S(2)}) async-start(bf16[32,2,16384]{2,1,0:T(2,128)(2,1)} %reshape.181), calls=%async_computation.2 | async-start | bytes 4194304 | tf_op jit(solution)/shard_map/all_to_all | solution.py:70
  144.7 52.9 %all-to-all-start.3 = ((bf16[32,2,16384]{2,1,0:T(2,128)(2,1)}), bf16[32,2,16384]{2,1,0:T(2,128)(2,1)}, u32[]{:S(2)}, u32[]{:S(2)}) async-start(bf16[32,2,16384]{2,1,0:T(2,128)(2,1)} %reshape.183), calls=%async_computation.3 | async-start | bytes 4194304 | tf_op jit(solution)/shard_map/all_to_all | solution.py:71
  148.9 255.0 %all-gather.4.cloned.1.call-start = ((), (), s32[]{:S(2)}) async-start(), calls=%async_computation.6 | async-start | bytes 4325376 | tf_op jit(solution)/shard_map/all_gather | solution.py:90
  330.3 11.2 %copy-start.10 = (f32[8,128]{1,0:T(8,128)S(1)}, f32[8,128]{1,0:T(8,128)}, u32[]{:S(2)}) copy-start(f32[8,128]{1,0:T(8,128)} %get-tuple-element.92) | copy-start | bytes 12292
  330.3 12.3 %copy-start.13 = (s32[8]{0:T(128)S(1)}, s32[8]{0:T(128)}, u32[]{:S(2)}) copy-start(s32[8]{0:T(128)} %param.21) | copy-start | bytes 100
  342.5 274.2 %reduce-scatter.3.cloned.1.call-start = ((), (), s32[]{:S(2)}) async-start(), calls=%async_computation.7 | async-start | bytes 8650752 | tf_op jit(solution)/shard_map/reduce_scatter | solution.py:128
  434.1 14.8 %copy-start.9 = (f32[2048]{0:T(1024)S(1)}, f32[2048]{0:T(1024)}, u32[]{:S(2)}) copy-start(f32[2048]{0:T(1024)} %param.24) | copy-start | bytes 24580
  448.9 10.4 %copy-start.5 = (bf16[2048,256]{1,0:T(8,128)(2,1)S(1)}, bf16[2048,256]{1,0:T(8,128)(2,1)}, u32[]{:S(2)}) copy-start(bf16[2048,256]{1,0:T(8,128)(2,1)} %param.25) | copy-start | bytes 3145732
  448.9 11.7 %copy-start.7 = (bf16[2048,256]{1,0:T(8,128)(2,1)S(1)}, bf16[2048,256]{1,0:T(8,128)(2,1)}, u32[]{:S(2)}) copy-start(bf16[2048,256]{1,0:T(8,128)(2,1)} %param.26) | copy-start | bytes 3145732
  459.3 3.5 copy-start.3
  461.9 1.0 copy-start.1
  462.9 4.6 copy-start.11
  467.4 205.2 %all-gather.6.cloned.1.call-start = ((), (), s32[]{:S(2)}) async-start(), calls=%async_computation.9 | async-start | bytes 2162688 | tf_op jit(solution)/shard_map/all_gather | solution.py:135
  509.1 0.8 copy-start.4
  510.1 110.4 %copy-start.12 = (s32[8]{0:T(128)S(1)}, s32[8]{0:T(128)}, u32[]{:S(2)}) copy-start(s32[8]{0:T(128)} %param.20) | copy-start | bytes 100
  620.4 232.9 %reduce-scatter.5.cloned.1.call-start = ((), (), s32[]{:S(2)}) async-start(), calls=%async_computation.8 | async-start | bytes 8650752 | tf_op jit(solution)/shard_map/reduce_scatter | solution.py:155
  693.2 5.1 copy-start.2
  693.2 5.1 copy-start.6
  698.3 1.5 copy-start.8
Sparse Core Ops, SparseCore 0:
  342.6 61.2 all-gather.3
  467.5 149.1 reduce-scatter.2
  620.5 52.0 all-gather.5
  704.6 148.6 reduce-scatter.4
